TPU v7x, 32 devices: a whole 2x2x4 slice. The times are simulated.
32 devices in a mesh: seq: 16 (over z, x, core), head: 2 (over y).
Axes of the slice: x: 2, y: 2, z: 4, core: 2. Of those that a mesh axis runs over, the one named last changes fastest.
Arguments:
- fw_query: bfloat16 [6144, 4096], P('seq', 'head'), may hold values from -6 to 6
- fw_key: bfloat16 [6144, 4096], P('seq', 'head'), may hold values from -6 to 6
- fw_value: bfloat16 [6144, 4096], P('seq', 'head'), may hold values from -6 to 6
- learn_rate: float32 [6144, 8], P('seq', 'head'), may hold values from 0.00025515517 to 0.002551552
- fast_weights: bfloat16 [3, 8, 512, 512], P(None, 'head'), may hold values from -0.25 to 0.25
- attn_query: bfloat16 [6144, 4096], P(('seq', 'head')), may hold values from -32 to 32
- attn_key: bfloat16 [6144, 1024], P(('seq', 'head')), may hold values from -32 to 32
- attn_value: bfloat16 [6144, 1024], P(('seq', 'head')), may hold values from -6 to 6
Outputs:
- mixed: bfloat16 [6144, 4096], P(('seq', 'head'))
All inputs are finite; a program needn't handle non-finite values.
Results may differ from a plain program's by a relative error of at most 0.01.
Values may be sent and summed in bfloat16 or wider, within the bound.
A program may use at most 128 MiB of HBM per device.

v0:
```python
import math

import jax
import jax.numpy as jnp
from jax import lax
from jax.sharding import PartitionSpec as P

Q_HEADS = 32
KV_HEADS = 8
HEAD_DIM = 128
WINDOW = 256


def shifted(value, axis, by):
    devices = lax.axis_size(axis)
    pairs = [(i, i + by) for i in range(devices) if 0 <= i + by < devices]
    return lax.ppermute(value, axis, pairs)


def local_grads(keys, values, rates, weights):
    pre_gate = jnp.einsum("thd,hde->the", keys, weights[0], preferred_element_type=jnp.float32)
    pre_up = jnp.einsum("thd,hde->the", keys, weights[1], preferred_element_type=jnp.float32)
    sigm = jax.nn.sigmoid(pre_gate)
    hidden = (pre_gate * sigm * pre_up).astype(jnp.bfloat16)
    scaled = (rates[:, :, None] * values.astype(jnp.float32)).astype(jnp.bfloat16)
    back = jnp.einsum("the,hde->thd", scaled, weights[2], preferred_element_type=jnp.float32)
    d_gate = (back * pre_up * sigm * (1.0 + pre_gate * (1.0 - sigm))).astype(jnp.bfloat16)
    d_up = (back * pre_gate * sigm).astype(jnp.bfloat16)
    grad_gate = jnp.einsum("thd,the->hde", keys, d_gate, preferred_element_type=jnp.float32)
    grad_up = jnp.einsum("thd,the->hde", keys, d_up, preferred_element_type=jnp.float32)
    grad_down = jnp.einsum("thd,the->hde", hidden, scaled, preferred_element_type=jnp.float32)
    return jnp.stack([grad_gate, grad_up, grad_down])


def renorm(summed, start_weights):
    start = start_weights.astype(jnp.float32)
    stepped = start + summed
    ratio = jnp.sqrt(jnp.mean(start * start, axis=-2, keepdims=True)) * lax.rsqrt(
        jnp.mean(stepped * stepped, axis=-2, keepdims=True) + 1e-06
    )
    return (stepped * ratio).astype(jnp.bfloat16)


def on_device(
    fw_query, fw_key, fw_value, learn_rate, fast_weights, attn_query, attn_key, attn_value
):
    tok_rows = fw_key.shape[0]
    local_heads = fast_weights.shape[1]
    width = fast_weights.shape[2]
    keys = fw_key.reshape(tok_rows, local_heads, width)
    values = fw_value.reshape(tok_rows, local_heads, width)
    queries = fw_query.reshape(tok_rows, local_heads, width)
    grads = local_grads(keys, values, learn_rate, fast_weights)
    share = lax.psum_scatter(grads, "seq", scatter_dimension=3, tiled=True)
    columns = share.shape[3]
    start_cols = lax.dynamic_slice_in_dim(fast_weights, lax.axis_index("seq") * columns, columns, 3)
    fresh_part = renorm(share, start_cols)
    fresh = lax.all_gather(fresh_part, "seq", axis=3, tiled=True)
    q_gate = jnp.einsum("thd,hde->the", queries, fresh[0], preferred_element_type=jnp.float32)
    q_up = jnp.einsum("thd,hde->the", queries, fresh[1], preferred_element_type=jnp.float32)
    answer_hidden = (q_gate * jax.nn.sigmoid(q_gate) * q_up).astype(jnp.bfloat16)
    fw_out = jnp.einsum(
        "the,hef->thf", answer_hidden, fresh[2], preferred_element_type=jnp.float32
    ).astype(jnp.bfloat16)
    fw_out = fw_out.reshape(tok_rows, local_heads * width)
    fw_fine = lax.all_to_all(fw_out, "head", split_axis=0, concat_axis=1, tiled=True)
    rows = attn_query.shape[0]
    reach = -(-WINDOW // rows)
    kv_width = attn_key.shape[1]
    group = Q_HEADS // KV_HEADS
    buffer_k = jnp.zeros(((reach + 1) * rows, kv_width), jnp.bfloat16)
    buffer_v = jnp.zeros(((reach + 1) * rows, kv_width), jnp.bfloat16)
    buffer_k = lax.dynamic_update_slice_in_dim(buffer_k, attn_key, reach * rows, 0)
    buffer_v = lax.dynamic_update_slice_in_dim(buffer_v, attn_value, reach * rows, 0)

    def bring(step, carry):
        piece_k, piece_v, store_k, store_v = carry
        piece_k, piece_v = shifted((piece_k, piece_v), ("seq", "head"), 1)
        slot = (reach - 1 - step) * rows
        store_k = lax.dynamic_update_slice_in_dim(store_k, piece_k, slot, 0)
        store_v = lax.dynamic_update_slice_in_dim(store_v, piece_v, slot, 0)
        return (piece_k, piece_v, store_k, store_v)

    carried = lax.fori_loop(0, reach, bring, (attn_key, attn_value, buffer_k, buffer_v))
    buffer_k = carried[2].reshape((reach + 1) * rows, KV_HEADS, HEAD_DIM)
    buffer_v = carried[3].reshape((reach + 1) * rows, KV_HEADS, HEAD_DIM)
    device_pos = lax.axis_index("seq") * lax.axis_size("head") + lax.axis_index("head")
    t_pos = device_pos * rows + jnp.arange(rows, dtype=jnp.int32)
    s_pos = (device_pos - reach) * rows + jnp.arange((reach + 1) * rows, dtype=jnp.int32)
    gap = t_pos[:, None] - s_pos[None, :]
    keep = (gap >= 0) & (gap < WINDOW) & (s_pos[None, :] >= 0)
    query_heads = attn_query.reshape(rows, KV_HEADS, group, HEAD_DIM)
    scaling = 1.0 / math.sqrt(HEAD_DIM)
    scores = (
        jnp.einsum("fcgd,lcd->cgfl", query_heads, buffer_k, preferred_element_type=jnp.float32)
        * scaling
    )
    scores = jnp.where(keep, scores, -1e30)
    top = jnp.max(scores, axis=-1, keepdims=True)
    expo = jnp.exp(scores - top)
    probs = (expo / jnp.sum(expo, axis=-1, keepdims=True)).astype(jnp.bfloat16)
    attn_out = jnp.einsum("cgfl,lcd->fcgd", probs, buffer_v, preferred_element_type=jnp.float32)
    attn_out = attn_out.reshape(rows, Q_HEADS * HEAD_DIM)
    return (attn_out + fw_fine.astype(jnp.float32)).astype(jnp.bfloat16)


def solution(mesh):
    placed = (
        P("seq", "head"),
        P("seq", "head"),
        P("seq", "head"),
        P("seq", "head"),
        P(None, "head", None, None),
        P(("seq", "head"), None),
        P(("seq", "head"), None),
        P(("seq", "head"), None),
    )
    return jax.shard_map(
        on_device, mesh=mesh, in_specs=placed, out_specs=P(("seq", "head"), None), check_vma=False
    )
```

profile of v0, /device:TPU:20, one launch (start us, length us, event | category | flops | bytes accessed | tf_op | source)
XLA Modules:
  0.0 307.9 jit_solution(8790722140409803399)
XLA Ops:
  10.2 3.2 %fusion.27 = f32[4,512,384]{1,2,0:T(8,128)S(1)} fusion(bf16[3,4,512,512]{3,2,1,0:T(8,128)(2,1)} %param.14, bf16[48,4,8,512]{3,2,1,0:T(8,128)(2,1)} %bitcast.163), kind=kOutput, calls=%fused_computation.49 | convolution fusion | flops 805306368 | bytes 6815744 | tf_op jit(solution)/shard_map/thd,hde->the/dot_general | solution.py:21
  19.0 3.8 %convolution_bitcast_fusion.2 = f32[1,4,512,512]{2,3,1,0:T(8,128)} fusion(f32[4,512,384]{1,2,0:T(8,128)S(1)} %fusion.27, f32[4,512,384]{1,2,0:T(8,128)S(1)} %fusion.29, f32[4,384,512]{2,1,0:T(8,128)S(1)} %fusion.31, bf16[48,4,8,512]{3,2,1,0:T(8,128)(2,1)S(1)} %bitcast.165), kind=kOutput, calls=%fused_computation.42 | convolution fusion | flops 813170688 | bytes 15204352 | tf_op jit(solution)/shard_map/thd,the->hde/dot_general | solution.py:29
  22.9 3.3 %convolution_bitcast_fusion.1 = f32[1,4,512,512]{2,3,1,0:T(8,128)} fusion(f32[4,512,384]{1,2,0:T(8,128)S(1)} %fusion.27, f32[4,384,512]{2,1,0:T(8,128)S(1)} %fusion.31, bf16[48,4,8,512]{3,2,1,0:T(8,128)(2,1)S(1)} %bitcast.166), kind=kOutput, calls=%fused_computation.41 | convolution fusion | flops 810024960 | bytes 12058624 | tf_op jit(solution)/shard_map/thd,the->hde/dot_general | solution.py:30
  26.2 9.5 %pad_maximum_fusion = f32[3,4,512,512]{2,3,1,0:T(8,128)} fusion(f32[1,4,512,512]{2,3,1,0:T(8,128)S(1)} %convolution_bitcast_fusion, f32[1,4,512,512]{2,3,1,0:T(8,128)} %convolution_bitcast_fusion.1, f32[1,4,512,512]{2,3,1,0:T(8,128)} %convolution_bitcast_fusion.2), kind=kLoop, calls=%fused_computation.6 | loop fusion | flops 6291456 | bytes 25165824 | tf_op jit(solution)/shard_map/stack | solution.py:32
  38.5 132.4 %reduce-scatter.2.cloned.1.call-done = f32[3,4,512,32]{2,3,1,0:T(8,128)} async-done(((f32[3,4,512,512]{2,3,1,0:T(8,128)}), f32[3,4,512,32]{2,3,1,0:T(8,128)}) %reduce-scatter.2.cloned.1.call-update) | async-done | bytes 786448 | tf_op jit(solution)/shard_map/reduce_scatter | solution.py:54
  172.3 2.0 multiply_convert_fusion
  176.4 2.2 dynamic_update_slice.21
  178.6 45.1 %while.19 = (s32[]{:T(128)}, bf16[192,1024]{1,0:T(8,128)(2,1)}, bf16[192,1024]{1,0:T(8,128)(2,1)}, bf16[576,1024]{1,0:T(8,128)(2,1)S(1)}, bf16[576,1024]{1,0:T(8...) while((s32[]{:T(128)}, bf16[192,1024]{1,0:T(8,128)(2,1)}, bf16[192,1024]{1,0:T(8,128)(2,1)}, ...), condition=%wide.region_1.0_spmd, body=%wide.region_0.0_spmd.sunk | while | flops 7 | bytes 6291695 | solution.py:84
  180.5 3.0 collective-permute-start.1
  183.5 9.1 %collective-permute-done = bf16[192,1024]{1,0:T(8,128)(2,1)S(1)} collective-permute-done((bf16[192,1024]{1,0:T(8,128)(2,1)}, bf16[192,1024]{1,0:T(8,128)(2,1)S(1)}, u32[]{:S(2)}, u32[]{:S(2)}) %collective-permute-start) | collective-permute-done | bytes 393248 | tf_op jit(solution)/shard_map/while/body/eval_jaxpr/ppermute | solution.py:17
  193.4 6.5 %collective-permute-done.1 = bf16[192,1024]{1,0:T(8,128)(2,1)S(1)} collective-permute-done((bf16[192,1024]{1,0:T(8,128)(2,1)}, bf16[192,1024]{1,0:T(8,128)(2,1)S(1)}, u32[]{:S(2)}, u32[]{:S(2)}) %collective-permute-start.1) | collective-permute-done | bytes 393248 | tf_op jit(solution)/shard_map/while/body/eval_jaxpr/ppermute | solution.py:17
  203.4 2.3 collective-permute-start.1
  205.7 12.1 %collective-permute-done = bf16[192,1024]{1,0:T(8,128)(2,1)S(1)} collective-permute-done((bf16[192,1024]{1,0:T(8,128)(2,1)}, bf16[192,1024]{1,0:T(8,128)(2,1)S(1)}, u32[]{:S(2)}, u32[]{:S(2)}) %collective-permute-start) | collective-permute-done | bytes 393248 | tf_op jit(solution)/shard_map/while/body/eval_jaxpr/ppermute | solution.py:17
  218.6 3.5 %collective-permute-done.1 = bf16[192,1024]{1,0:T(8,128)(2,1)S(1)} collective-permute-done((bf16[192,1024]{1,0:T(8,128)(2,1)}, bf16[192,1024]{1,0:T(8,128)(2,1)S(1)}, u32[]{:S(2)}, u32[]{:S(2)}) %collective-permute-start.1) | collective-permute-done | bytes 393248 | tf_op jit(solution)/shard_map/while/body/eval_jaxpr/ppermute | solution.py:17
  225.0 3.9 %reshape.61 = bf16[192,8,4,128]{3,2,1,0:T(4,128)(2,1)} reshape(bf16[192,4096]{1,0:T(8,128)(2,1)} %param.15) | data formatting | bytes 3145728 | tf_op jit(solution)/shard_map/reshape | solution.py:92
  230.6 11.4 %fusion.76 = (f32[8,4,192]{2,1,0:T(4,128)S(1)}, f32[8,4,192,576]{3,2,1,0:T(8,128)}) fusion(pred[192,576]{1,0:T(8,128)(4,1)S(1)} %fusion.67, bf16[192,8,4,128]{3,2,1,0:T(4,128)(2,1)} %reshape.61, bf16[576,8,128,1]{2,1,0,3:T(8,128)(2,1)} %bitcast.170), kind=kOutput, calls=%fused_computation.95 | convolution fusion | flops 920126016 | bytes 17043456 | tf_op jit(solution)/shard_map/sub | solution.py:100
  242.0 2.7 all-gather.2.cloned.1.call-done
  244.7 4.3 %fusion.24 = f32[4,512,384]{1,2,0:T(8,128)} fusion(bf16[384,4,512]{0,2,1:T(8,128)(2,1)S(1)} %bitcast.161, bf16[3,4,512,512]{2,3,1,0:T(8,128)(2,1)} %all-gather.2.cloned.1.call-done), kind=kOutput, calls=%fused_computation.44 | convolution fusion | flops 805306368 | bytes 6815744 | tf_op jit(solution)/shard_map/thd,hde->the/dot_general | solution.py:60
  249.0 5.5 %fusion.46 = bf16[384,4,512]{0,2,1:T(8,128)(2,1)S(1)} fusion(f32[4,512,384]{1,2,0:T(8,128)} %fusion.24, bf16[384,4,512]{0,2,1:T(8,128)(2,1)S(1)} %bitcast.162, bf16[3,4,512,512]{2,3,1,0:T(8,128)(2,1)} %all-gather.2.cloned.1.call-done), kind=kOutput, calls=%fused_computation.64 | convolution fusion | flops 1616117760 | bytes 10485760 | tf_op jit(solution)/shard_map/the,hef->thf/dot_general | solution.py:62
  256.1 2.4 all_to_all.10
  258.5 25.6 %all-to-all-start = ((bf16[2,192,2048]{2,1,0:T(8,128)(2,1)}), bf16[2,192,2048]{2,1,0:T(8,128)(2,1)}, u32[]{:S(2)}, u32[]{:S(2)}) async-start(bf16[2,192,2048]{2,1,0:T(8,128)(2,1)} %all_to_all.10), calls=%async_computation.1 | async-start | bytes 3145728 | tf_op jit(solution)/shard_map/all_to_all | solution.py:66
  284.1 6.9 %fusion.36 = f32[192,8,4,128]{3,0,2,1:T(8,128)S(1)} fusion(f32[8,4,192,576]{3,2,1,0:T(8,128)} %get-tuple-element.115, f32[8,4,192]{2,1,0:T(4,128)S(1)} %get-tuple-element.114, bf16[576,8,128,1]{2,1,0,3:T(8,128)(2,1)S(1)} %bitcast.169), kind=kOutput, calls=%fused_computation.58 | convolution fusion | flops 913047552 | bytes 18505728 | tf_op jit(solution)/shard_map/cgfl,lcd->fcgd/dot_general | solution.py:102
  291.0 2.0 copy.32
  293.1 2.8 reshape.62
  (53 shorter events, 33.6 us)
Async XLA Ops:
  6.5 164.4 %reduce-scatter.2.cloned.1.call-start = ((), (), s32[]{:S(2)}) async-start(), calls=%async_computation.2 | async-start | bytes 13369344 | tf_op jit(solution)/shard_map/reduce_scatter | solution.py:54
  6.5 6.9 %copy-start.2 = (bf16[384,2048]{1,0:T(8,128)(2,1)S(1)}, bf16[384,2048]{1,0:T(8,128)(2,1)}, u32[]{:S(2)}) copy-start(bf16[384,2048]{1,0:T(8,128)(2,1)} %param.11) | copy-start | bytes 4718596
  10.2 3.9 %copy-start.1 = (bf16[3,4,512,512]{3,2,1,0:T(8,128)(2,1)S(1)}, bf16[3,4,512,512]{3,2,1,0:T(8,128)(2,1)}, u32[]{:S(2)}) copy-start(bf16[3,4,512,512]{3,2,1,0:T(8,128)(2,1)} %param.14) | copy-start | bytes 18874372
  14.1 1.4 copy-start.5
  15.5 0.7 copy-start.7
  35.7 209.0 %all-gather.2.cloned.1.call-start = ((), (), s32[]{:S(2)}) async-start(), calls=%async_computation.3 | async-start | bytes 6684672 | tf_op jit(solution)/shard_map/all_gather | solution.py:58
  37.8 136.5 %copy-start.4 = (bf16[384,2048]{1,0:T(8,128)(2,1)S(1)}, bf16[384,2048]{1,0:T(8,128)(2,1)}, u32[]{:S(2)}) copy-start(bf16[384,2048]{1,0:T(8,128)(2,1)} %param.10) | copy-start | bytes 4718596
  178.6 14.1 %collective-permute-start = (bf16[192,1024]{1,0:T(8,128)(2,1)}, bf16[192,1024]{1,0:T(8,128)(2,1)S(1)}, u32[]{:S(2)}, u32[]{:S(2)}) collective-permute-start(bf16[192,1024]{1,0:T(8,128)(2,1)} %get-tuple-element.157), channel_id=1, source_target_pairs={{0,1},{1,2},{2,3},{3,4},{4,5},{5,6},{6,7},{7,8},{8,9},{9,10},{10,1... | collective-permute-start | bytes 1179656 | tf_op jit(solution)/shard_map/while/body/eval_jaxpr/ppermute | solution.py:17
  180.5 19.4 %collective-permute-start.1 = (bf16[192,1024]{1,0:T(8,128)(2,1)}, bf16[192,1024]{1,0:T(8,128)(2,1)S(1)}, u32[]{:S(2)}, u32[]{:S(2)}) collective-permute-start(bf16[192,1024]{1,0:T(8,128)(2,1)} %get-tuple-element.158), channel_id=1, source_target_pairs={{0,1},{1,2},{2,3},{3,4},{4,5},{5,6},{6,7},{7,8},{8,9},{9,10},{10,1... | collective-permute-start | bytes 1179656 | tf_op jit(solution)/shard_map/while/body/eval_jaxpr/ppermute | solution.py:17
  201.5 16.3 %collective-permute-start = (bf16[192,1024]{1,0:T(8,128)(2,1)}, bf16[192,1024]{1,0:T(8,128)(2,1)S(1)}, u32[]{:S(2)}, u32[]{:S(2)}) collective-permute-start(bf16[192,1024]{1,0:T(8,128)(2,1)} %get-tuple-element.157), channel_id=1, source_target_pairs={{0,1},{1,2},{2,3},{3,4},{4,5},{5,6},{6,7},{7,8},{8,9},{9,10},{10,1... | collective-permute-start | bytes 1179656 | tf_op jit(solution)/shard_map/while/body/eval_jaxpr/ppermute | solution.py:17
  203.4 18.6 %collective-permute-start.1 = (bf16[192,1024]{1,0:T(8,128)(2,1)}, bf16[192,1024]{1,0:T(8,128)(2,1)S(1)}, u32[]{:S(2)}, u32[]{:S(2)}) collective-permute-start(bf16[192,1024]{1,0:T(8,128)(2,1)} %get-tuple-element.158), channel_id=1, source_target_pairs={{0,1},{1,2},{2,3},{3,4},{4,5},{5,6},{6,7},{7,8},{8,9},{9,10},{10,1... | collective-permute-start | bytes 1179656 | tf_op jit(solution)/shard_map/while/body/eval_jaxpr/ppermute | solution.py:17
  225.0 3.9 %copy-start.3 = (bf16[576,1024]{1,0:T(8,128)(2,1)S(1)}, bf16[576,1024]{1,0:T(8,128)(2,1)}, u32[]{:S(2)}) copy-start(bf16[576,1024]{1,0:T(8,128)(2,1)} %get-tuple-element.100) | copy-start | bytes 3538948
  256.1 28.0 %copy-start.6 = (bf16[72,8,8,128]{3,2,1,0:T(8,128)(2,1)S(1)}, bf16[72,8,8,128]{3,2,1,0:T(8,128)(2,1)}, u32[]{:S(2)}) copy-start(bf16[72,8,8,128]{3,2,1,0:T(8,128)(2,1)} %copy.72) | copy-start | bytes 3538948
  258.5 37.5 %all-to-all-start = ((bf16[2,192,2048]{2,1,0:T(8,128)(2,1)}), bf16[2,192,2048]{2,1,0:T(8,128)(2,1)}, u32[]{:S(2)}, u32[]{:S(2)}) async-start(bf16[2,192,2048]{2,1,0:T(8,128)(2,1)} %all_to_all.10), calls=%async_computation.1 | async-start | bytes 3145728 | tf_op jit(solution)/shard_map/all_to_all | solution.py:66
  297.7 1.9 copy-start
Sparse Core Ops, SparseCore 0:
  35.8 135.0 reduce-scatter.1
  174.5 70.1 all-gather.1
where the time goes:
time: 309 us; the launch traced here: 308 us
  waiting for transfers between devices  166 us (54%)
  matrix products  42.3 us (14%)
  starting transfers between devices  35 us (11%)
  local copies, waits for them, and re-layouts  33.8 us (11%)
  other arithmetic  16.8 us (5%)
  between operations  13.6 us (4%)
    reduce_scatter x1, waiting for transfers between devices, on_device(): share = lax.psum_scatter(grads, 'seq', scatter_dimension=3, tiled=True)  132 us
    ppermute x4, waiting for transfers between devices, shifted(): return lax.ppermute(value, axis, pairs)  31.2 us
    all_to_all x1, starting transfers between devices, on_device(): lax.all_to_all(fw_out, 'head', split_axis=0, concat_axis=1, tiled=True)  25.6 us
    sub x1, matrix products, on_device(): expo = jnp.exp(scores - top)  11.4 us
    unnamed x21, local copies, waits for them, and re-layouts  10.2 us
    another operation x1, other arithmetic, local_grads(): return jnp.stack([grad_gate, grad_up, grad_down])  9.52 us
    ppermute x4, starting transfers between devices, shifted(): return lax.ppermute(value, axis, pairs)  9.11 us
    dot_general x1, matrix products, on_device(): jnp.einsum('cgfl,lcd->fcgd', probs, buffer_v, preferred_element_type=jnp....  6.93 us
  transfers between devices with their start and end apart: 7, of which 6 were waited for; matrix products, arithmetic and copies ran while one was open for 13% of the time, Pallas kernels for 0%

commit v1 on v0

--- a/solution.py
+++ b/solution.py
@@ -1,8 +1,11 @@
+import functools
 import math
 
 import jax
 import jax.numpy as jnp
 from jax import lax
+from jax.experimental import pallas as pl
+from jax.experimental.pallas import tpu as pltpu
 from jax.sharding import PartitionSpec as P
 
 Q_HEADS = 32
@@ -103,6 +106,479 @@
     attn_out = attn_out.reshape(rows, Q_HEADS * HEAD_DIM)
     return (attn_out + fw_fine.astype(jnp.float32)).astype(jnp.bfloat16)
 
+MESH = pl.DeviceIdType.MESH
+LANES = 128
+
+
+def gray(i):
+    return i + (i // 2) * (1 - 2 * (i % 2))
+
+
+def fused_kernel(
+    heads, width, rows,
+    q_hbm, k_hbm, v_hbm, rate_ref, w_hbm, aq_hbm, ak_hbm, av_hbm, out_ref,
+    qb, kb, vb, wb, aqb, akb, avb, g, r0, r1, r2, r3, nw, att, bias, fsend, frecv,
+    in_sem, misc_sem, halo_s, halo_r, s0_s, s0_r, s1_s, s1_r, s2_s, s2_r, s3_s, s3_r,
+    za_s, za_r, zb_s, zb_r, x_s, x_r, c_s, c_r, y_s, y_r,
+):
+    me = lax.axis_index("seq")
+    y = lax.axis_index("head")
+    n_seq, n_head = lax.axis_size("seq"), lax.axis_size("head")
+    core, xx, zb0, zb1 = me % 2, (me // 2) % 2, (me // 4) % 2, me // 8
+    z = me // 4
+    cb = core * 2 + xx
+    other_core = me + 1 - 2 * core
+    other_x = me + 2 - 4 * xx
+    z_near = me + 4 - 8 * zb0
+    z_far = me + 8 - 16 * zb1
+    pos = me * n_head + y
+    last = n_seq * n_head
+    extra = WINDOW - rows
+    pad = akb.shape[0] - WINDOW - rows
+
+    def cols(block, size=LANES):
+        return pl.ds(pl.multiple_of(block * size, size), size)
+
+    def remote(src, dst, ssem, rsem, seq, head=None):
+        return pltpu.make_async_remote_copy(
+            src_ref=src, dst_ref=dst, send_sem=ssem, recv_sem=rsem,
+            device_id={"seq": seq, "head": y if head is None else head},
+            device_id_type=MESH,
+        )
+
+    def loads(h):
+        c = cols(h, width)
+        return (
+            pltpu.make_async_copy(k_hbm.at[:, c], kb.at[:, c], in_sem.at[h, 0]),
+            pltpu.make_async_copy(v_hbm.at[:, c], vb.at[:, c], in_sem.at[h, 1]),
+            pltpu.make_async_copy(w_hbm.at[:, h], wb.at[:, h], in_sem.at[h, 2]),
+        )
+
+    own_at = pl.ds(pad + WINDOW, rows)
+    others = (
+        pltpu.make_async_copy(aq_hbm, aqb, misc_sem.at[0]),
+        pltpu.make_async_copy(ak_hbm, akb.at[own_at], misc_sem.at[1]),
+        pltpu.make_async_copy(av_hbm, avb.at[own_at], misc_sem.at[2]),
+        pltpu.make_async_copy(q_hbm, qb, misc_sem.at[3]),
+    )
+    for i in range(heads):
+        for copy in loads(i + (i // 2) * (1 - 2 * (i % 2))):
+            copy.start()
+    for copy in others:
+        copy.start()
+
+    barrier = pltpu.get_barrier_semaphore()
+
+    def greet(seq, head):
+        pl.semaphore_signal(barrier, inc=1, device_id={"seq": seq, "head": head}, device_id_type=MESH)
+
+    for seq in (other_core, other_x, z_near, z_far):
+        greet(seq, y)
+    greet(me, 1 - y)
+
+    for step in (1, 2):
+        for there in (pos + step, pos + last - step):
+            there = there % last
+            greet(there // n_head, there % n_head)
+    pl.semaphore_wait(barrier, 9)
+
+    def halo(step):
+        there = pos + step
+        seq, head = there // n_head, there % n_head
+        if step == 1:
+            src, dst = pl.ds(0, rows), pl.ds(pad + extra, rows)
+        else:
+            src, dst = pl.ds(rows - extra, extra), pl.ds(pad, extra)
+        j = (step - 1) * 2
+        return (
+            remote(ak_hbm.at[src], akb.at[dst], halo_s.at[j], halo_r.at[j], seq, head),
+            remote(av_hbm.at[src], avb.at[dst], halo_s.at[j + 1], halo_r.at[j + 1], seq, head),
+        )
+
+    for step in (1, 2):
+        @pl.when(pos + step < last)
+        def _():
+            for copy in halo(step):
+                copy.start()
+
+        @pl.when(pos < step)
+        def _():
+            at = pl.ds(pad + extra, rows) if step == 1 else pl.ds(pad, extra)
+            akb[at, :] = jnp.zeros((at.size, akb.shape[1]), akb.dtype)
+            avb[at, :] = jnp.zeros((at.size, avb.shape[1]), avb.dtype)
+
+    akb[pl.ds(0, pad), :] = jnp.zeros((pad, akb.shape[1]), akb.dtype)
+    avb[pl.ds(0, pad), :] = jnp.zeros((pad, avb.shape[1]), avb.dtype)
+    t_idx = lax.broadcasted_iota(jnp.int32, bias.shape, 0)
+    s_idx = lax.broadcasted_iota(jnp.int32, bias.shape, 1) - (pad + WINDOW)
+    gap = t_idx - s_idx
+    keep = (gap >= 0) & (gap < WINDOW) & (s_idx + pos * rows >= 0)
+    bias[...] = keep.astype(jnp.float32)
+
+    def s0(h, m):
+        return remote(
+            g.at[h, m, :, cols(1 - core, 2 * LANES)], r0.at[h, m], s0_s.at[h, m], s0_r.at[h, m], other_core
+        )
+
+    def s1(h, m):
+        return remote(
+            g.at[h, m, :, cols(core * 2 + 1 - xx)], r1.at[h, m], s1_s.at[h, m], s1_r.at[h, m], other_x
+        )
+
+    def s2(h, m):
+        return remote(
+            g.at[h, m, :, cols(cb)], r2.at[h // 2, m], s2_s.at[h // 2, m], s2_r.at[h // 2, m], z_near
+        )
+
+    def s3(h, m):
+        return remote(g.at[h, m, :, cols(cb)], r3.at[m], s3_s.at[m], s3_r.at[m], z_far)
+
+    def add(h, m, block, piece):
+        mine = g[h, m, :, cols(block)].astype(jnp.float32)
+        g[h, m, :, cols(block)] = (mine + piece.astype(jnp.float32)).astype(g.dtype)
+
+    def compute(h):
+        for copy in loads(h):
+            copy.wait()
+        c = cols(h, width)
+        keys = kb[:, c]
+        head_lane = lax.broadcasted_iota(jnp.int32, rate_ref.shape, 1)
+        rate = jnp.sum(jnp.where(head_lane == h, rate_ref[...], 0.0), axis=1, keepdims=True)
+        scaled = (rate * vb[:, c].astype(jnp.float32)).astype(jnp.bfloat16)
+        pre_gate = jnp.dot(keys, wb[0, h], preferred_element_type=jnp.float32)
+        pre_up = jnp.dot(keys, wb[1, h], preferred_element_type=jnp.float32)
+        sigm = jax.nn.sigmoid(pre_gate)
+        hidden = (pre_gate * sigm * pre_up).astype(jnp.bfloat16)
+        tn = (((0,), (0,)), ((), ()))
+
+        def put(m, left, right):
+            g[h, m] = lax.dot_general(left, right, tn, preferred_element_type=jnp.float32).astype(g.dtype)
+            s0(h, m).start()
+
+        put(2, hidden, scaled)
+        back = lax.dot_general(
+            scaled, wb[2, h], (((1,), (1,)), ((), ())), preferred_element_type=jnp.float32
+        )
+        d_up = (back * pre_gate * sigm).astype(jnp.bfloat16)
+        put(1, keys, d_up)
+        d_gate = (back * pre_up * sigm * (1.0 + pre_gate * (1.0 - sigm))).astype(jnp.bfloat16)
+        put(0, keys, d_gate)
+
+    def first_add(h):
+        def one(j, _):
+            m = 2 - j
+            s0(h, m).wait_recv()
+            add(h, m, core * 2 + 1 - xx, r0[h, m, :, cols(1 - xx)])
+            s1(h, m).start()
+            add(h, m, cb, r0[h, m, :, cols(xx)])
+            return 0
+
+        lax.fori_loop(0, 3, one, 0)
+
+    def loop_a(i, _):
+        compute(gray(i))
+
+        @pl.when(i > 0)
+        def _():
+            first_add(gray(i - 1))
+
+        return 0
+
+    lax.fori_loop(0, heads, loop_a, 0)
+    first_add(gray(heads - 1))
+
+    group = Q_HEADS // KV_HEADS
+    scaling = 1.0 / math.sqrt(HEAD_DIM)
+
+    def attend(c):
+        keys = akb[:, cols(c)]
+        vals = avb[:, cols(c)]
+        for j in range(group):
+            qc = cols(c * group + j)
+            scores = lax.dot_general(
+                aqb[:, qc], keys, (((1,), (1,)), ((), ())), preferred_element_type=jnp.float32
+            ) * scaling
+            scores = jnp.where(bias[...] > 0.0, scores, -1e30)
+            top = jnp.max(scores, axis=-1, keepdims=True)
+            expo = jnp.exp(scores - top)
+            probs = (expo / jnp.sum(expo, axis=-1, keepdims=True)).astype(jnp.bfloat16)
+            att[:, qc] = jnp.dot(probs, vals, preferred_element_type=jnp.float32)
+
+    for copy in others:
+        copy.wait()
+    for step in (1, 2):
+        @pl.when(pos >= step)
+        def _():
+            for copy in halo(step):
+                copy.wait_recv()
+
+    def share(h, m, block):
+        return nw.at[h, m, :, cols(block)]
+
+    def far(h, m):
+        return remote(share(h, m, cb), share(h, m, cb), za_s.at[m], za_r.at[m], z_far)
+
+    def near(h, m):
+        b = h // 2
+        return remote(share(h, m, cb), share(h, m, cb), zb_s.at[b, m], zb_r.at[b, m], z_near)
+
+    def near_from(h, m):
+        return near(h, m)
+
+    def side(h, m):
+        return remote(share(h, m, cb), share(h, m, cb), x_s.at[h, m], x_r.at[h, m], other_x)
+
+    def pair(h, m, x_of):
+        block = core * 2 + x_of
+        return remote(
+            share(h, m, block), share(h, m, block), c_s.at[h, m, x_of], c_r.at[h, m, x_of], other_core
+        )
+
+    def side_from(h, m):
+        block = core * 2 + 1 - xx
+        return remote(share(h, m, block), share(h, m, block), x_s.at[h, m], x_r.at[h, m], other_x)
+
+    def pair_from(h, m, x_of):
+        block = (1 - core) * 2 + x_of
+        return remote(
+            share(h, m, block), share(h, m, block), c_s.at[h, m, x_of], c_r.at[h, m, x_of], other_core
+        )
+
+    def stage2(p):
+        h, m = gray(p // 3), 2 - p % 3
+        s1(h, m).wait_recv()
+        add(h, m, cb, r1[h, m])
+
+        @pl.when(h % 2 != zb0)
+        def _():
+            s2(h, m).start()
+
+    def stage3(p):
+        h, m = gray(p // 3), 2 - p % 3
+
+        @pl.when(h % 2 == zb0)
+        def _():
+            s2(h, m).wait_recv()
+            add(h, m, cb, r2[h // 2, m])
+
+            @pl.when(h // 2 != zb1)
+            def _():
+                s3(h, m).start()
+
+    def stage4(p):
+        h, m = gray(p // 3), 2 - p % 3
+
+        @pl.when(h == z)
+        def _():
+            s3(h, m).wait_recv()
+            start = wb[m, h, :, cols(cb)].astype(jnp.float32)
+            total = g[h, m, :, cols(cb)].astype(jnp.float32) + r3[m].astype(jnp.float32)
+            stepped = start + total
+            ratio = jnp.sqrt(jnp.mean(start * start, axis=0, keepdims=True)) * lax.rsqrt(
+                jnp.mean(stepped * stepped, axis=0, keepdims=True) + 1e-06
+            )
+            nw[h, m, :, cols(cb)] = (stepped * ratio).astype(nw.dtype)
+            side(h, m).start()
+            far(h, m).start()
+            near(h, m).start()
+            pair(h, m, xx).start()
+
+    pieces = heads * 3
+
+    def loop_b(t, _):
+        @pl.when(t < pieces)
+        def _():
+            stage2(t)
+
+        @pl.when((t >= 1) & (t < pieces + 1))
+        def _():
+            stage3(t - 1)
+
+        @pl.when(t >= 2)
+        def _():
+            stage4(t - 2)
+
+        @pl.when(t < KV_HEADS)
+        def _():
+            attend(t)
+
+        return 0
+
+    lax.fori_loop(0, pieces + 2, loop_b, 0)
+
+    def answer_send(h):
+        return remote(fsend.at[h], frecv.at[h], y_s.at[h], y_r.at[h], me, 1 - y)
+
+    def head_of(i):
+        return ((zb1 + i % 2) % 2) * 2 + (zb0 + i // 2) % 2
+
+    def mix(value, group_of, h):
+        at = cols(group_of * heads + h, width)
+        out_ref[:, at] = (att[:, at] + value.astype(jnp.float32)).astype(out_ref.dtype)
+
+    def loop_c(i, _):
+        h = head_of(i)
+
+        @pl.when(i == 0)
+        def _():
+            def one(j, _):
+                m = 2 - j
+                h_far = head_of(1)
+                far(h_far, m).wait_recv()
+                near(h_far, m).start()
+                side(h_far, m).start()
+                pair(h_far, m, xx).start()
+                return 0
+
+            lax.fori_loop(0, 3, one, 0)
+
+        @pl.when(i < 2)
+        def _():
+            def one(j, _):
+                m = 2 - j
+                h_near = head_of(i + 2)
+                near_from(h_near, m).wait_recv()
+                side(h_near, m).start()
+                pair(h_near, m, xx).start()
+                return 0
+
+            lax.fori_loop(0, 3, one, 0)
+
+        def crossed(j, _):
+            m = 2 - j
+            side_from(h, m).wait_recv()
+            pair(h, m, 1 - xx).start()
+            return 0
+
+        lax.fori_loop(0, 3, crossed, 0)
+
+        def landed(m, _):
+            pair_from(h, m, 0).wait_recv()
+            pair_from(h, m, 1).wait_recv()
+            return 0
+
+        lax.fori_loop(0, 3, landed, 0)
+        queries = qb[:, cols(h, width)]
+        q_gate = jnp.dot(queries, nw[h, 0], preferred_element_type=jnp.float32)
+        q_up = jnp.dot(queries, nw[h, 1], preferred_element_type=jnp.float32)
+        hid = (q_gate * jax.nn.sigmoid(q_gate) * q_up).astype(jnp.bfloat16)
+        full = jnp.dot(hid, nw[h, 2], preferred_element_type=jnp.float32).astype(jnp.bfloat16)
+        low, high = full[:rows], full[rows:]
+        lower = jnp.zeros((rows, width), jnp.int32) + y < 1
+        fsend[h] = jnp.where(lower, high.astype(jnp.float32), low.astype(jnp.float32)).astype(jnp.bfloat16)
+        answer_send(h).start()
+        mix(jnp.where(lower, low.astype(jnp.float32), high.astype(jnp.float32)), y, h)
+        return 0
+
+    lax.fori_loop(0, heads, loop_c, 0)
+
+    def loop_d(i, _):
+        h = head_of(i)
+        answer_send(h).wait_recv()
+        mix(frecv[h], 1 - y, h)
+        return 0
+
+    lax.fori_loop(0, heads, loop_d, 0)
+
+    for step in (1, 2):
+        @pl.when(pos + step < last)
+        def _():
+            for copy in halo(step):
+                copy.wait_send()
+
+    def sent(p, _):
+        h, m = p // 3, p % 3
+        s0(h, m).wait_send()
+        s1(h, m).wait_send()
+
+        @pl.when(h % 2 != zb0)
+        def _():
+            s2(h, m).wait_send()
+
+        @pl.when((h % 2 == zb0) & (h // 2 != zb1))
+        def _():
+            s3(h, m).wait_send()
+
+        @pl.when(h == z)
+        def _():
+            far(h, m).wait_send()
+
+        @pl.when(h % 2 == zb0)
+        def _():
+            near(h, m).wait_send()
+
+        side(h, m).wait_send()
+        pair(h, m, 0).wait_send()
+        pair(h, m, 1).wait_send()
+        return 0
+
+    lax.fori_loop(0, pieces, sent, 0)
+
+    def sent_y(h, _):
+        answer_send(h).wait_send()
+        return 0
+
+    lax.fori_loop(0, heads, sent_y, 0)
+
+
+def fused(fw_query, fw_key, fw_value, learn_rate, fast_weights, attn_query, attn_key, attn_value):
+    tokens, heads, width = fw_key.shape[0], fast_weights.shape[1], fast_weights.shape[2]
+    rows, kv_width = attn_key.shape
+    span = -(-(WINDOW + rows) // LANES) * LANES
+    bf, f32 = jnp.bfloat16, jnp.float32
+    anywhere = pl.BlockSpec(memory_space=pl.ANY)
+    vmem = pl.BlockSpec(memory_space=pltpu.VMEM)
+    dma = pltpu.SemaphoreType.DMA
+    half = heads // 2
+    return pl.pallas_call(
+        functools.partial(fused_kernel, heads, width, rows),
+        out_shape=jax.ShapeDtypeStruct(attn_query.shape, bf),
+        in_specs=[anywhere, anywhere, anywhere, vmem, anywhere, anywhere, anywhere, anywhere],
+        out_specs=vmem,
+        scratch_shapes=[
+            pltpu.VMEM(fw_query.shape, bf),
+            pltpu.VMEM(fw_key.shape, bf),
+            pltpu.VMEM(fw_value.shape, bf),
+            pltpu.VMEM(fast_weights.shape, bf),
+            pltpu.VMEM(attn_query.shape, bf),
+            pltpu.VMEM((span, kv_width), bf),
+            pltpu.VMEM((span, kv_width), bf),
+            pltpu.VMEM((heads, 3, width, width), bf),
+            pltpu.VMEM((heads, 3, width, 2 * LANES), bf),
+            pltpu.VMEM((heads, 3, width, LANES), bf),
+            pltpu.VMEM((half, 3, width, LANES), bf),
+            pltpu.VMEM((3, width, LANES), bf),
+            pltpu.VMEM((heads, 3, width, width), bf),
+            pltpu.VMEM(attn_query.shape, f32),
+            pltpu.VMEM((rows, span), f32),
+            pltpu.VMEM((heads, rows, width), bf),
+            pltpu.VMEM((heads, rows, width), bf),
+            dma((heads, 3)), dma((4,)), dma((4,)), dma((4,)),
+            dma((heads, 3)), dma((heads, 3)), dma((heads, 3)), dma((heads, 3)),
+            dma((half, 3)), dma((half, 3)), dma((3,)), dma((3,)),
+            dma((3,)), dma((3,)), dma((half, 3)), dma((half, 3)),
+            dma((heads, 3)), dma((heads, 3)), dma((heads, 3, 2)), dma((heads, 3, 2)),
+            dma((heads,)), dma((heads,)),
+        ],
+        compiler_params=pltpu.CompilerParams(
+            collective_id=0, has_side_effects=True, vmem_limit_bytes=60 * 1024 * 1024
+        ),
+    )(fw_query, fw_key, fw_value, learn_rate, fast_weights, attn_query, attn_key, attn_value)
+
+
+def takes_fused(mesh, args):
+    tokens, rows = args[1].shape[0], args[5].shape[0]
+    heads, width = args[4].shape[1], args[4].shape[2]
+    return (
+        mesh.shape["seq"] == 16
+        and mesh.shape["head"] == 2
+        and heads == 4
+        and width == 4 * LANES
+        and tokens == 2 * rows
+        and rows < WINDOW < 2 * rows
+        and (-(WINDOW + rows)) % LANES > 0
+    )
+
 
 def solution(mesh):
     placed = (
@@ -115,6 +591,10 @@
         P(("seq", "head"), None),
         P(("seq", "head"), None),
     )
+
+    def body(*args):
+        return fused(*args) if takes_fused(mesh, args) else on_device(*args)
+
     return jax.shard_map(
-        on_device, mesh=mesh, in_specs=placed, out_specs=P(("seq", "head"), None), check_vma=False
+        body, mesh=mesh, in_specs=placed, out_specs=P(("seq", "head"), None), check_vma=False
     )

time: 309 us -> 134 us (0.43)
  the two profiles are of different devices: /device:TPU:20 before, /device:TPU:3 now
where the time goes in v1:
time: 134 us; the launch traced here: 133 us
  Pallas kernels  129 us (96%)
  local copies, waits for them, and re-layouts  4.21 us (3%)
    pallas_call x1, Pallas kernels, fused(): pl.pallas_call(functools.partial(fused_kernel, heads, width, rows), out_s...  129 us
    unnamed x2, local copies, waits for them, and re-layouts  4.21 us

profile of v1, /device:TPU:3, one launch (start us, length us, event | category | flops | bytes accessed | tf_op | source)
XLA Modules:
  0.0 133.3 jit_solution(1784894414673280292)
XLA Ops:
  0.0 1.5 %copy.9.rate_ref = f32[384,4]{1,0:T(8,128)} copy(f32[384,4]{0,1:T(4,128)} %param.11) | data formatting | bytes 12288 | tf_op args[3]
  1.5 129.1 %shard_map.82 = bf16[192,4096]{1,0:T(8,128)(2,1)} custom-call(bf16[384,2048]{1,0:T(8,128)(2,1)} %q_hbm.1, bf16[384,2048]{1,0:T(8,128)(2,1)} %k_hbm.1, bf16[384,2048]{1,0:T(8,128)(2,1)} %v_hbm.1, f32[384,4]{1,0:T(8,128)} %copy.9.rate_ref, bf16[3,4,512,512]{3,2,1,0:T(8,128)(2,1)} %w_hbm.1, bf16[192,4096]{1,0:T(8,128)(2,1)} %aq_hbm.1, ...), custom_call_target="tpu_custom_call" | custom-call | tf_op jit(solution)/shard_map/pallas_call | solution.py:533
  130.6 2.7 %copy.11 = bf16[192,4096]{1,0:T(8,128)(2,1)} copy(bf16[192,4096]{1,0:T(8,128)(2,1)} %shard_map.82) | data formatting | bytes 3145728

commit v2 on v1

--- a/solution.py
+++ b/solution.py
@@ -304,14 +304,6 @@
             probs = (expo / jnp.sum(expo, axis=-1, keepdims=True)).astype(jnp.bfloat16)
             att[:, qc] = jnp.dot(probs, vals, preferred_element_type=jnp.float32)
 
-    for copy in others:
-        copy.wait()
-    for step in (1, 2):
-        @pl.when(pos >= step)
-        def _():
-            for copy in halo(step):
-                copy.wait_recv()
-
     def share(h, m, block):
         return nw.at[h, m, :, cols(block)]
 
@@ -384,27 +376,39 @@
             pair(h, m, xx).start()
 
     pieces = heads * 3
+    first_att = 4
+    lag3, lag4 = 5, 10
 
     def loop_b(t, _):
         @pl.when(t < pieces)
         def _():
             stage2(t)
 
-        @pl.when((t >= 1) & (t < pieces + 1))
-        def _():
-            stage3(t - 1)
-
-        @pl.when(t >= 2)
-        def _():
-            stage4(t - 2)
-
-        @pl.when(t < KV_HEADS)
-        def _():
-            attend(t)
+        @pl.when((t >= lag3) & (t < pieces + lag3))
+        def _():
+            stage3(t - lag3)
+
+        @pl.when(t >= lag4)
+        def _():
+            stage4(t - lag4)
+
+        @pl.when(t == first_att)
+        def _():
+            for copy in others:
+                copy.wait()
+            for step in (1, 2):
+                @pl.when(pos >= step)
+                def _():
+                    for copy in halo(step):
+                        copy.wait_recv()
+
+        @pl.when((t >= first_att) & (t < first_att + KV_HEADS))
+        def _():
+            attend(t - first_att)
 
         return 0
 
-    lax.fori_loop(0, pieces + 2, loop_b, 0)
+    lax.fori_loop(0, pieces + lag4, loop_b, 0)
 
     def answer_send(h):
         return remote(fsend.at[h], frecv.at[h], y_s.at[h], y_r.at[h], me, 1 - y)

time: 134 us -> 117 us (0.87)
  the two profiles are of different devices: /device:TPU:3 before, /device:TPU:27 now
where the time goes in v2:
time: 117 us; the launch traced here: 116 us
  Pallas kernels  112 us (96%)
  local copies, waits for them, and re-layouts  4.21 us (4%)
    pallas_call x1, Pallas kernels, fused(): pl.pallas_call(functools.partial(fused_kernel, heads, width, rows), out_s...  112 us
    unnamed x2, local copies, waits for them, and re-layouts  4.21 us

profile of v2, /device:TPU:27, one launch (start us, length us, event | category | flops | bytes accessed | tf_op | source)
XLA Modules:
  0.0 116.4 jit_solution(2201192868195300095)
XLA Ops:
  0.0 1.5 %copy.9.rate_ref = f32[384,4]{1,0:T(8,128)} copy(f32[384,4]{0,1:T(4,128)} %param.11) | data formatting | bytes 12288 | tf_op args[3]
  1.5 112.2 %shard_map.82 = bf16[192,4096]{1,0:T(8,128)(2,1)} custom-call(bf16[384,2048]{1,0:T(8,128)(2,1)} %q_hbm.1, bf16[384,2048]{1,0:T(8,128)(2,1)} %k_hbm.1, bf16[384,2048]{1,0:T(8,128)(2,1)} %v_hbm.1, f32[384,4]{1,0:T(8,128)} %copy.9.rate_ref, bf16[3,4,512,512]{3,2,1,0:T(8,128)(2,1)} %w_hbm.1, bf16[192,4096]{1,0:T(8,128)(2,1)} %aq_hbm.1, ...), custom_call_target="tpu_custom_call" | custom-call | tf_op jit(solution)/shard_map/pallas_call | solution.py:537
  113.7 2.7 %copy.11 = bf16[192,4096]{1,0:T(8,128)(2,1)} copy(bf16[192,4096]{1,0:T(8,128)(2,1)} %shard_map.82) | data formatting | bytes 3145728
